TPU v7x, 32 devices: a whole 2x2x4 slice. The times are simulated.
32 devices in a mesh: slab: 8 (over z, x), row: 4 (over y, core).
Axes of the slice: x: 2, y: 2, z: 4, core: 2. Of those that a mesh axis runs over, the one named last changes fastest.
Arguments:
- edge_weights: int32 [3, 16, 32, 512], P(None, 'slab', 'row'), may hold values from 1 to 15
- seeds: int32 [16, 32, 512], P('slab', 'row'), may hold values from -8 to 7
- supervoxel: int32 [16, 32, 512], P('slab', 'row'), may hold values from 0 to 127
- coarse_blocks: float32 [4, 1024, 1024], P('row', 'slab'), as said below
Outputs:
- potentials: float32 [8, 16, 32, 512], P(None, 'slab', 'row')
Inputs may be any that keep to these rules, and one draw needn't show every extreme that they name: `seeds`: a negative value marks an unseeded voxel. `coarse_blocks`: the entries named by dc lie between 0.6 and 1.2 times 2 * 8 * 4.
All inputs are finite; a program needn't handle non-finite values.
Results may differ from a plain program's by a relative error of at most 0.00024.
Values sent between devices are 32-bit elements; how exact they have to be, the bound alone decides.
No kernel may reach another device: no remote copies, remote signals or barrier semaphores. Data moves between devices by JAX's collectives and lax.ppermute only.
A program may use at most 64 MiB of HBM per device.

v0:
```python
import math
import jax
import jax.numpy as jnp
from jax import lax
from jax.sharding import PartitionSpec as P

LABELS = 8
CZ = 2
CY = 8
NX = 512
CC = 128
CYCLES = 2
prior_mass = 0.25
seed_weight = 4.0
smooth_step = 0.8
coarse_step = 0.7
weight_unit = 0.125


def padded(cells, sides, width):
    for axis, dim in sides:
        count = lax.axis_size(axis)
        ends = count - 1
        head = lax.slice_in_dim(cells, 0, width, axis=dim)
        tail = lax.slice_in_dim(cells, cells.shape[dim] - width, cells.shape[dim], axis=dim)
        cells = jnp.concatenate(
            [
                lax.ppermute(tail, axis, [(i, (i + 1) % count) for i in range(ends)]),
                cells,
                lax.ppermute(head, axis, [((i + 1) % count, i) for i in range(ends)]),
            ],
            axis=dim,
        )
    return cells


def shifted(block, axis, distance):
    devices = range(lax.axis_size(axis))
    route = [(i - distance, i) for i in devices if i - distance in devices]
    return lax.ppermute(block, axis, route)


def lower_x(a):
    return jnp.pad(a[..., :-1], [(0, 0)] * (a.ndim - 1) + [(1, 0)])


def upper_x(a):
    return jnp.pad(a[..., 1:], [(0, 0)] * (a.ndim - 1) + [(0, 1)])


def crop(a, margin):
    return a[..., margin : a.shape[-3] - margin, margin : a.shape[-2] - margin, :]


def rim_one(field):
    return padded(field, (("slab", 1), ("row", 2)), 1)


def per_device(edge_weights, seeds, supervoxel, coarse_blocks):
    n_slab = lax.axis_size("slab")
    n_row = lax.axis_size("row")
    group = min(16, n_slab)
    sections = n_slab // group
    slab_pos = lax.axis_index("slab")
    row_pos = lax.axis_index("row")
    stacked = jnp.concatenate([edge_weights, seeds[None]], axis=0)
    lower_plane = shifted(edge_weights[0, -1:], "slab", 1)
    lower_row = shifted(edge_weights[1, :, -1:], "row", 1)
    framed = jnp.pad(stacked, ((0, 0), (1, 1), (1, 1), (0, 0)))
    framed = framed.at[0, :1, 1:-1].set(lower_plane)
    framed = framed.at[1, 1:-1, :1].set(lower_row)
    width = (framed.shape[1] - CZ) // 2
    weights = framed[:3].astype(jnp.float32) * weight_unit
    plane_ids = slab_pos * CZ - width + jnp.arange(CZ + 2 * width, dtype=jnp.int32)
    line_ids = row_pos * CY - width + jnp.arange(CY + 2 * width, dtype=jnp.int32)
    keep_z = (plane_ids != CZ * n_slab - 1).astype(jnp.float32)[:, None, None]
    keep_y = (line_ids != CY * n_row - 1).astype(jnp.float32)[None, :, None]
    keep_x = (jnp.arange(NX) < NX - 1).astype(jnp.float32)[None, None, :]
    w_z = weights[0] * keep_z
    w_y = weights[1] * keep_y
    w_x = weights[2] * keep_x
    seed_inner = crop(framed[3], 1)
    inner_x = crop(w_x, 1)
    diag = (
        prior_mass
        + seed_weight * (seed_inner >= 0).astype(jnp.float32)
        + crop(w_z, 1)
        + crop(w_y, 1)
        + inner_x
        + w_z[:-2, 1:-1]
        + w_y[1:-1, :-2]
        + lower_x(inner_x)
    )
    label_ids = jnp.arange(LABELS, dtype=jnp.int32)
    source = seed_weight * (seed_inner[None] == label_ids[:, None, None, None]).astype(jnp.float32)

    def residual_on(frame, rim):
        margin = width - rim - 1
        face_z = crop(w_z, margin)
        face_y = crop(w_y, margin)
        face_x = crop(w_x, margin)[1:-1, 1:-1]
        centre = frame[:, 1:-1, 1:-1]
        near = face_z[1:-1, 1:-1] * frame[:, 2:, 1:-1] + face_z[:-2, 1:-1] * frame[:, :-2, 1:-1]
        near = (
            near + face_y[1:-1, 1:-1] * frame[:, 1:-1, 2:] + face_y[1:-1, :-2] * frame[:, 1:-1, :-2]
        )
        near = near + face_x * upper_x(centre) + lower_x(face_x) * lower_x(centre)
        local_diag = crop(diag, width - 1 - rim)
        local_source = crop(source, width - 1 - rim)
        return (local_source - (local_diag * centre - near), local_diag, centre)

    def sweep(field):
        change, local_diag, centre = residual_on(rim_one(field), 0)
        return centre + smooth_step * change / local_diag

    block_row = coarse_blocks[0]
    turn = slab_pos // sections
    section_id = slab_pos % sections
    own_block = lax.dynamic_slice_in_dim(block_row, turn * CC, CC, 1)
    coarse_diag = jnp.diagonal(own_block)
    cells = CZ * CY * NX
    span = math.gcd(cells, 2048)
    flat_ids = supervoxel.reshape(cells)
    coarse_ids = jnp.arange(CC, dtype=jnp.int32)
    field = jnp.zeros((LABELS, CZ, CY, NX), jnp.float32)
    for cycle in range(CYCLES):
        field = sweep(sweep(field))
        residual, unused_diag, unused_centre = residual_on(rim_one(field), 0)
        flat_rows = residual.reshape(LABELS, cells)

        def collect_block(index, total):
            piece = lax.dynamic_slice_in_dim(flat_rows, index * span, span, 1)
            piece_ids = lax.dynamic_slice_in_dim(flat_ids, index * span, span, 0)
            onehot = (piece_ids[:, None] == coarse_ids[None, :]).astype(jnp.float32)
            return total + jnp.dot(
                piece, onehot, precision=lax.Precision.HIGHEST, preferred_element_type=jnp.float32
            )

        coarse_rhs = lax.fori_loop(
            0, cells // span, collect_block, jnp.zeros((LABELS, CC), jnp.float32)
        )
        first = coarse_step * coarse_rhs / coarse_diag
        gathered = lax.all_gather(first, "slab", axis=1, tiled=True)
        arranged = gathered.reshape(LABELS, group, sections, CC)
        section = lax.dynamic_slice_in_dim(arranged, section_id, 1, 2).reshape(LABELS, group * CC)
        second = (
            first
            + coarse_step
            * (
                coarse_rhs
                - lax.dot_general(
                    section,
                    block_row,
                    (((1,), (1,)), ((), ())),
                    precision=lax.Precision.HIGHEST,
                    preferred_element_type=jnp.float32,
                )
            )
            / coarse_diag
        )
        correction = jnp.take(second, flat_ids, axis=1).reshape(LABELS, CZ, CY, NX)
        field = sweep(field + correction)
    return field


def solution(mesh):
    in_specs = (
        P(None, "slab", "row", None),
        P("slab", "row", None),
        P("slab", "row", None),
        P("row", "slab", None),
    )
    out_specs = P(None, "slab", "row", None)
    return jax.shard_map(
        per_device, mesh=mesh, in_specs=in_specs, out_specs=out_specs, check_vma=False
    )
```

profile of v0, /device:TPU:6, one launch (start us, length us, event | category | flops | bytes accessed | tf_op | source)
XLA Modules:
  0.0 296.9 jit_solution(196694166765577341)
XLA Ops:
  0.0 2.6 collective-permute-start.2
  2.6 4.3 %collective-permute-start.3 = (f32[8,1,8,512]{3,2,1,0:T(8,128)S(1)}, f32[8,1,8,512]{3,2,1,0:T(8,128)S(1)}, u32[]{:S(2)}, u32[]{:S(2)}) collective-permute-start(f32[8,1,8,512]{3,2,1,0:T(8,128)S(1)} %broadcast.145), channel_id=1, source_target_pairs={{0,4},{4,8},{8,12},{12,16},{16,20},{20,24},{24,28},{1,5},{5,9},{9,... | collective-permute-start | bytes 393224 | tf_op jit(solution)/shard_map/ppermute | solution.py:28
  7.6 2.5 collective-permute-start
  16.7 3.6 %collective-permute-start.4 = (f32[8,4,1,512]{3,2,1,0:T(1,128)S(1)}, f32[8,4,1,512]{3,2,1,0:T(1,128)S(1)}, u32[]{:S(2)}, u32[]{:S(2)}) collective-permute-start(f32[8,4,1,512]{3,2,1,0:T(1,128)S(1)} %get-tuple-element.286), channel_id=1, source_target_pairs={{1,0},{2,1},{3,2},{5,4},{6,5},{7,6},{9,8},{10,9},{11,10},{13,12},{... | collective-permute-start | bytes 196616 | tf_op jit(solution)/shard_map/ppermute | solution.py:30
  22.4 3.6 %collective-permute-done.5 = f32[8,4,1,512]{3,2,1,0:T(1,128)S(1)} collective-permute-done((f32[8,4,1,512]{3,2,1,0:T(1,128)S(1)}, f32[8,4,1,512]{3,2,1,0:T(1,128)S(1)}, u32[]{:S(2)}, u32[]{:S(2)}) %collective-permute-start.5) | collective-permute-done | bytes 65568 | tf_op jit(solution)/shard_map/ppermute | solution.py:28
  26.2 3.3 %collective-permute-start.6 = (f32[8,1,8,512]{3,2,1,0:T(8,128)S(1)}, f32[8,1,8,512]{3,2,1,0:T(8,128)S(1)}, u32[]{:S(2)}, u32[]{:S(2)}) collective-permute-start(f32[8,1,8,512]{3,2,1,0:T(8,128)S(1)} %get-tuple-element.318), channel_id=1, source_target_pairs={{4,0},{8,4},{12,8},{16,12},{20,16},{24,20},{28,24},{5,1},{9,5},{13... | collective-permute-start | bytes 393224 | tf_op jit(solution)/shard_map/ppermute | solution.py:30
  29.5 3.5 %collective-permute-start.7 = (f32[8,1,8,512]{3,2,1,0:T(8,128)S(1)}, f32[8,1,8,512]{3,2,1,0:T(8,128)S(1)}, u32[]{:S(2)}, u32[]{:S(2)}) collective-permute-start(f32[8,1,8,512]{3,2,1,0:T(8,128)S(1)} %get-tuple-element.317), channel_id=1, source_target_pairs={{0,4},{4,8},{8,12},{12,16},{16,20},{20,24},{24,28},{1,5},{5,9},{9,... | collective-permute-start | bytes 393224 | tf_op jit(solution)/shard_map/ppermute | solution.py:28
  41.0 3.0 %collective-permute-done.9 = f32[8,4,1,512]{3,2,1,0:T(1,128)S(1)} collective-permute-done((f32[8,4,1,512]{3,2,1,0:T(1,128)S(1)}, f32[8,4,1,512]{3,2,1,0:T(1,128)S(1)}, u32[]{:S(2)}, u32[]{:S(2)}) %collective-permute-start.9) | collective-permute-done | bytes 65568 | tf_op jit(solution)/shard_map/ppermute | solution.py:28
  46.2 4.8 %collective-permute-start.11 = (f32[8,1,8,512]{3,2,1,0:T(8,128)S(1)}, f32[8,1,8,512]{3,2,1,0:T(8,128)S(1)}, u32[]{:S(2)}, u32[]{:S(2)}) collective-permute-start(f32[8,1,8,512]{3,2,1,0:T(8,128)S(1)} %get-tuple-element.313), channel_id=1, source_target_pairs={{0,4},{4,8},{8,12},{12,16},{16,20},{20,24},{24,28},{1,5},{5,9},{9,... | collective-permute-start | bytes 393224 | tf_op jit(solution)/shard_map/ppermute | solution.py:28
  58.1 3.0 %collective-permute-done.13 = f32[8,4,1,512]{3,2,1,0:T(1,128)S(1)} collective-permute-done((f32[8,4,1,512]{3,2,1,0:T(1,128)S(1)}, f32[8,4,1,512]{3,2,1,0:T(1,128)S(1)}, u32[]{:S(2)}, u32[]{:S(2)}) %collective-permute-start.13) | collective-permute-done | bytes 65568 | tf_op jit(solution)/shard_map/ppermute | solution.py:28
  61.6 2.5 while.30
  64.1 31.9 %all_gather.6 = f32[8,1024]{1,0:T(8,128)S(1)} all-gather(f32[8,128]{1,0:T(8,128)S(1)} %multiply_divide_fusion.1), channel_id=1, replica_groups=mesh['slab'=8,'row'=4] {'slab'}, dimensions={1}, use_global_device_ids=true | all-gather | bytes 36864 | tf_op jit(solution)/shard_map/all_gather | solution.py:143
  96.6 27.9 %gather_fusion.1 = f32[8192,8]{1,0:T(8,128)} fusion(f32[8,128]{0,1:T(8,128)S(1)} %copy.9, s32[8192]{0:T(1024)S(1)} %fusion.122), kind=kCustom, calls=%fused_computation.clone | custom fusion | bytes 557056 | tf_op jit(solution)/shard_map/jit(_take)/gather | solution.py:161
  124.5 7.5 %broadcast_select_fusion.1 = f32[8192,8]{1,0:T(8,128)} fusion(f32[8192,8]{1,0:T(8,128)} %gather_fusion.1, pred[8192]{0:T(1024)(128)(4,1)S(1)} %compare_and_fusion), kind=kLoop, calls=%fused_computation.16 | loop fusion | flops 65536 | bytes 532480 | tf_op jit(solution)/shard_map/jit(_take)/select_n | solution.py:161
  131.9 2.8 copy.10
  134.8 3.3 %collective-permute-start.14 = (f32[8,1,8,512]{3,2,1,0:T(8,128)S(1)}, f32[8,1,8,512]{3,2,1,0:T(8,128)S(1)}, u32[]{:S(2)}, u32[]{:S(2)}) collective-permute-start(f32[8,1,8,512]{3,2,1,0:T(8,128)S(1)} %get-tuple-element.310), channel_id=1, source_target_pairs={{4,0},{8,4},{12,8},{16,12},{20,16},{24,20},{28,24},{5,1},{9,5},{13... | collective-permute-start | bytes 393224 | tf_op jit(solution)/shard_map/ppermute | solution.py:30
  138.1 3.5 %collective-permute-start.15 = (f32[8,1,8,512]{3,2,1,0:T(8,128)S(1)}, f32[8,1,8,512]{3,2,1,0:T(8,128)S(1)}, u32[]{:S(2)}, u32[]{:S(2)}) collective-permute-start(f32[8,1,8,512]{3,2,1,0:T(8,128)S(1)} %get-tuple-element.309), channel_id=1, source_target_pairs={{0,4},{4,8},{8,12},{12,16},{16,20},{20,24},{24,28},{1,5},{5,9},{9,... | collective-permute-start | bytes 393224 | tf_op jit(solution)/shard_map/ppermute | solution.py:28
  149.6 3.0 %collective-permute-done.17 = f32[8,4,1,512]{3,2,1,0:T(1,128)S(1)} collective-permute-done((f32[8,4,1,512]{3,2,1,0:T(1,128)S(1)}, f32[8,4,1,512]{3,2,1,0:T(1,128)S(1)}, u32[]{:S(2)}, u32[]{:S(2)}) %collective-permute-start.17) | collective-permute-done | bytes 65568 | tf_op jit(solution)/shard_map/ppermute | solution.py:28
  154.8 4.8 %collective-permute-start.19 = (f32[8,1,8,512]{3,2,1,0:T(8,128)S(1)}, f32[8,1,8,512]{3,2,1,0:T(8,128)S(1)}, u32[]{:S(2)}, u32[]{:S(2)}) collective-permute-start(f32[8,1,8,512]{3,2,1,0:T(8,128)S(1)} %get-tuple-element.305), channel_id=1, source_target_pairs={{0,4},{4,8},{8,12},{12,16},{16,20},{20,24},{24,28},{1,5},{5,9},{9,... | collective-permute-start | bytes 393224 | tf_op jit(solution)/shard_map/ppermute | solution.py:28
  166.7 3.0 %collective-permute-done.21 = f32[8,4,1,512]{3,2,1,0:T(1,128)S(1)} collective-permute-done((f32[8,4,1,512]{3,2,1,0:T(1,128)S(1)}, f32[8,4,1,512]{3,2,1,0:T(1,128)S(1)}, u32[]{:S(2)}, u32[]{:S(2)}) %collective-permute-start.21) | collective-permute-done | bytes 65568 | tf_op jit(solution)/shard_map/ppermute | solution.py:28
  172.0 5.3 %collective-permute-start.23 = (f32[8,1,8,512]{3,2,1,0:T(8,128)S(1)}, f32[8,1,8,512]{3,2,1,0:T(8,128)S(1)}, u32[]{:S(2)}, u32[]{:S(2)}) collective-permute-start(f32[8,1,8,512]{3,2,1,0:T(8,128)S(1)} %get-tuple-element.301), channel_id=1, source_target_pairs={{0,4},{4,8},{8,12},{12,16},{16,20},{20,24},{24,28},{1,5},{5,9},{9,... | collective-permute-start | bytes 393224 | tf_op jit(solution)/shard_map/ppermute | solution.py:28
  184.4 3.0 %collective-permute-done.25 = f32[8,4,1,512]{3,2,1,0:T(1,128)S(1)} collective-permute-done((f32[8,4,1,512]{3,2,1,0:T(1,128)S(1)}, f32[8,4,1,512]{3,2,1,0:T(1,128)S(1)}, u32[]{:S(2)}, u32[]{:S(2)}) %collective-permute-start.25) | collective-permute-done | bytes 65568 | tf_op jit(solution)/shard_map/ppermute | solution.py:28
  189.7 5.2 %collective-permute-start.27 = (f32[8,1,8,512]{3,2,1,0:T(8,128)S(1)}, f32[8,1,8,512]{3,2,1,0:T(8,128)S(1)}, u32[]{:S(2)}, u32[]{:S(2)}) collective-permute-start(f32[8,1,8,512]{3,2,1,0:T(8,128)S(1)} %get-tuple-element.297), channel_id=1, source_target_pairs={{0,4},{4,8},{8,12},{12,16},{16,20},{20,24},{24,28},{1,5},{5,9},{9,... | collective-permute-start | bytes 393224 | tf_op jit(solution)/shard_map/ppermute | solution.py:28
  202.0 3.0 %collective-permute-done.29 = f32[8,4,1,512]{3,2,1,0:T(1,128)S(1)} collective-permute-done((f32[8,4,1,512]{3,2,1,0:T(1,128)S(1)}, f32[8,4,1,512]{3,2,1,0:T(1,128)S(1)}, u32[]{:S(2)}, u32[]{:S(2)}) %collective-permute-start.29) | collective-permute-done | bytes 65568 | tf_op jit(solution)/shard_map/ppermute | solution.py:28
  205.5 2.5 while.31
  208.0 30.0 %all_gather.7 = f32[8,1024]{1,0:T(8,128)S(1)} all-gather(f32[8,128]{1,0:T(8,128)S(1)} %multiply_divide_fusion), channel_id=1, replica_groups=mesh['slab'=8,'row'=4] {'slab'}, dimensions={1}, use_global_device_ids=true | all-gather | bytes 36864 | tf_op jit(solution)/shard_map/all_gather | solution.py:143
  238.6 27.9 %gather_fusion.2 = f32[8192,8]{1,0:T(8,128)} fusion(f32[8,128]{0,1:T(8,128)S(1)} %copy.11, s32[8192]{0:T(1024)S(1)} %fusion.122), kind=kCustom, calls=%fused_computation.1.clone | custom fusion | bytes 557056 | tf_op jit(solution)/shard_map/jit(_take)/gather | solution.py:161
  266.5 7.5 %broadcast_select_fusion = f32[8192,8]{1,0:T(8,128)} fusion(f32[8192,8]{1,0:T(8,128)} %gather_fusion.2, pred[8192]{0:T(1024)(128)(4,1)S(1)} %compare_and_fusion), kind=kLoop, calls=%fused_computation.15 | loop fusion | flops 65536 | bytes 532480 | tf_op jit(solution)/shard_map/jit(_take)/select_n | solution.py:161
  273.9 2.8 copy.12
  276.8 4.6 %collective-permute-start.30 = (f32[8,1,8,512]{3,2,1,0:T(8,128)S(1)}, f32[8,1,8,512]{3,2,1,0:T(8,128)S(1)}, u32[]{:S(2)}, u32[]{:S(2)}) collective-permute-start(f32[8,1,8,512]{3,2,1,0:T(8,128)S(1)} %get-tuple-element.294), channel_id=1, source_target_pairs={{4,0},{8,4},{12,8},{16,12},{20,16},{24,20},{28,24},{5,1},{9,5},{13... | collective-permute-start | bytes 393224 | tf_op jit(solution)/shard_map/ppermute | solution.py:30
  284.6 3.7 %collective-permute-done.31 = f32[8,1,8,512]{3,2,1,0:T(8,128)S(1)} collective-permute-done((f32[8,1,8,512]{3,2,1,0:T(8,128)S(1)}, f32[8,1,8,512]{3,2,1,0:T(8,128)S(1)}, u32[]{:S(2)}, u32[]{:S(2)}) %collective-permute-start.31) | collective-permute-done | bytes 131104 | tf_op jit(solution)/shard_map/ppermute | solution.py:28
  292.9 3.0 %collective-permute-done.33 = f32[8,4,1,512]{3,2,1,0:T(1,128)S(1)} collective-permute-done((f32[8,4,1,512]{3,2,1,0:T(1,128)S(1)}, f32[8,4,1,512]{3,2,1,0:T(1,128)S(1)}, u32[]{:S(2)}, u32[]{:S(2)}) %collective-permute-start.33) | collective-permute-done | bytes 65568 | tf_op jit(solution)/shard_map/ppermute | solution.py:28
  (131 shorter events, 78.0 us)
Async XLA Ops:
  0.0 16.5 %collective-permute-start.2 = (f32[8,1,8,512]{3,2,1,0:T(8,128)S(1)}, f32[8,1,8,512]{3,2,1,0:T(8,128)S(1)}, u32[]{:S(2)}, u32[]{:S(2)}) collective-permute-start(f32[8,1,8,512]{3,2,1,0:T(8,128)S(1)} %broadcast.145), channel_id=1, source_target_pairs={{4,0},{8,4},{12,8},{16,12},{20,16},{24,20},{28,24},{5,1},{9,5},{13... | collective-permute-start | bytes 393224 | tf_op jit(solution)/shard_map/ppermute | solution.py:30
  2.6 14.0 %collective-permute-start.3 = (f32[8,1,8,512]{3,2,1,0:T(8,128)S(1)}, f32[8,1,8,512]{3,2,1,0:T(8,128)S(1)}, u32[]{:S(2)}, u32[]{:S(2)}) collective-permute-start(f32[8,1,8,512]{3,2,1,0:T(8,128)S(1)} %broadcast.145), channel_id=1, source_target_pairs={{0,4},{4,8},{8,12},{12,16},{16,20},{20,24},{24,28},{1,5},{5,9},{9,... | collective-permute-start | bytes 393224 | tf_op jit(solution)/shard_map/ppermute | solution.py:28
  7.6 8.4 %collective-permute-start = (s32[1,8,512]{2,1,0:T(8,128)S(1)}, s32[1,8,512]{2,1,0:T(8,128)S(1)}, u32[]{:S(2)}, u32[]{:S(2)}) collective-permute-start(s32[1,8,512]{2,1,0:T(8,128)S(1)} %slice_bitcast_fusion.4), channel_id=1, source_target_pairs={{0,4},{4,8},{8,12},{12,16},{16,20},{20,24},{24,28},{1,5},{5,9},{9,... | collective-permute-start | bytes 49160 | tf_op jit(solution)/shard_map/ppermute | solution.py:40
  10.9 5.3 %collective-permute-start.1 = (s32[2,1,512]{2,1,0:T(1,128)S(1)}, s32[2,1,512]{2,1,0:T(1,128)S(1)}, u32[]{:S(2)}, u32[]{:S(2)}) collective-permute-start(s32[2,1,512]{2,1,0:T(1,128)S(1)} %slice_bitcast_fusion.5), channel_id=1, source_target_pairs={{0,1},{1,2},{2,3},{4,5},{5,6},{6,7},{8,9},{9,10},{10,11},{12,13},{... | collective-permute-start | bytes 12296 | tf_op jit(solution)/shard_map/ppermute | solution.py:40
  16.7 5.7 %collective-permute-start.4 = (f32[8,4,1,512]{3,2,1,0:T(1,128)S(1)}, f32[8,4,1,512]{3,2,1,0:T(1,128)S(1)}, u32[]{:S(2)}, u32[]{:S(2)}) collective-permute-start(f32[8,4,1,512]{3,2,1,0:T(1,128)S(1)} %get-tuple-element.286), channel_id=1, source_target_pairs={{1,0},{2,1},{3,2},{5,4},{6,5},{7,6},{9,8},{10,9},{11,10},{13,12},{... | collective-permute-start | bytes 196616 | tf_op jit(solution)/shard_map/ppermute | solution.py:30
  20.3 5.6 %collective-permute-start.5 = (f32[8,4,1,512]{3,2,1,0:T(1,128)S(1)}, f32[8,4,1,512]{3,2,1,0:T(1,128)S(1)}, u32[]{:S(2)}, u32[]{:S(2)}) collective-permute-start(f32[8,4,1,512]{3,2,1,0:T(1,128)S(1)} %get-tuple-element.287), channel_id=1, source_target_pairs={{0,1},{1,2},{2,3},{4,5},{5,6},{6,7},{8,9},{9,10},{10,11},{12,13},{... | collective-permute-start | bytes 196616 | tf_op jit(solution)/shard_map/ppermute | solution.py:28
  26.2 7.9 %collective-permute-start.6 = (f32[8,1,8,512]{3,2,1,0:T(8,128)S(1)}, f32[8,1,8,512]{3,2,1,0:T(8,128)S(1)}, u32[]{:S(2)}, u32[]{:S(2)}) collective-permute-start(f32[8,1,8,512]{3,2,1,0:T(8,128)S(1)} %get-tuple-element.318), channel_id=1, source_target_pairs={{4,0},{8,4},{12,8},{16,12},{20,16},{24,20},{28,24},{5,1},{9,5},{13... | collective-permute-start | bytes 393224 | tf_op jit(solution)/shard_map/ppermute | solution.py:30
  29.5 6.9 %collective-permute-start.7 = (f32[8,1,8,512]{3,2,1,0:T(8,128)S(1)}, f32[8,1,8,512]{3,2,1,0:T(8,128)S(1)}, u32[]{:S(2)}, u32[]{:S(2)}) collective-permute-start(f32[8,1,8,512]{3,2,1,0:T(8,128)S(1)} %get-tuple-element.317), channel_id=1, source_target_pairs={{0,4},{4,8},{8,12},{12,16},{16,20},{20,24},{24,28},{1,5},{5,9},{9,... | collective-permute-start | bytes 393224 | tf_op jit(solution)/shard_map/ppermute | solution.py:28
  36.5 4.5 %collective-permute-start.8 = (f32[8,4,1,512]{3,2,1,0:T(1,128)S(1)}, f32[8,4,1,512]{3,2,1,0:T(1,128)S(1)}, u32[]{:S(2)}, u32[]{:S(2)}) collective-permute-start(f32[8,4,1,512]{3,2,1,0:T(1,128)S(1)} %get-tuple-element.284), channel_id=1, source_target_pairs={{1,0},{2,1},{3,2},{5,4},{6,5},{7,6},{9,8},{10,9},{11,10},{13,12},{... | collective-permute-start | bytes 196616 | tf_op jit(solution)/shard_map/ppermute | solution.py:30
  38.4 5.6 %collective-permute-start.9 = (f32[8,4,1,512]{3,2,1,0:T(1,128)S(1)}, f32[8,4,1,512]{3,2,1,0:T(1,128)S(1)}, u32[]{:S(2)}, u32[]{:S(2)}) collective-permute-start(f32[8,4,1,512]{3,2,1,0:T(1,128)S(1)} %get-tuple-element.285), channel_id=1, source_target_pairs={{0,1},{1,2},{2,3},{4,5},{5,6},{6,7},{8,9},{9,10},{10,11},{12,13},{... | collective-permute-start | bytes 196616 | tf_op jit(solution)/shard_map/ppermute | solution.py:28
  44.3 7.8 %collective-permute-start.10 = (f32[8,1,8,512]{3,2,1,0:T(8,128)S(1)}, f32[8,1,8,512]{3,2,1,0:T(8,128)S(1)}, u32[]{:S(2)}, u32[]{:S(2)}) collective-permute-start(f32[8,1,8,512]{3,2,1,0:T(8,128)S(1)} %get-tuple-element.314), channel_id=1, source_target_pairs={{4,0},{8,4},{12,8},{16,12},{20,16},{24,20},{28,24},{5,1},{9,5},{13... | collective-permute-start | bytes 393224 | tf_op jit(solution)/shard_map/ppermute | solution.py:30
  46.2 7.3 %collective-permute-start.11 = (f32[8,1,8,512]{3,2,1,0:T(8,128)S(1)}, f32[8,1,8,512]{3,2,1,0:T(8,128)S(1)}, u32[]{:S(2)}, u32[]{:S(2)}) collective-permute-start(f32[8,1,8,512]{3,2,1,0:T(8,128)S(1)} %get-tuple-element.313), channel_id=1, source_target_pairs={{0,4},{4,8},{8,12},{12,16},{16,20},{20,24},{24,28},{1,5},{5,9},{9,... | collective-permute-start | bytes 393224 | tf_op jit(solution)/shard_map/ppermute | solution.py:28
  53.6 4.5 %collective-permute-start.12 = (f32[8,4,1,512]{3,2,1,0:T(1,128)S(1)}, f32[8,4,1,512]{3,2,1,0:T(1,128)S(1)}, u32[]{:S(2)}, u32[]{:S(2)}) collective-permute-start(f32[8,4,1,512]{3,2,1,0:T(1,128)S(1)} %get-tuple-element.282), channel_id=1, source_target_pairs={{1,0},{2,1},{3,2},{5,4},{6,5},{7,6},{9,8},{10,9},{11,10},{13,12},{... | collective-permute-start | bytes 196616 | tf_op jit(solution)/shard_map/ppermute | solution.py:30
  55.6 5.6 %collective-permute-start.13 = (f32[8,4,1,512]{3,2,1,0:T(1,128)S(1)}, f32[8,4,1,512]{3,2,1,0:T(1,128)S(1)}, u32[]{:S(2)}, u32[]{:S(2)}) collective-permute-start(f32[8,4,1,512]{3,2,1,0:T(1,128)S(1)} %get-tuple-element.283), channel_id=1, source_target_pairs={{0,1},{1,2},{2,3},{4,5},{5,6},{6,7},{8,9},{9,10},{10,11},{12,13},{... | collective-permute-start | bytes 196616 | tf_op jit(solution)/shard_map/ppermute | solution.py:28
  134.8 7.8 %collective-permute-start.14 = (f32[8,1,8,512]{3,2,1,0:T(8,128)S(1)}, f32[8,1,8,512]{3,2,1,0:T(8,128)S(1)}, u32[]{:S(2)}, u32[]{:S(2)}) collective-permute-start(f32[8,1,8,512]{3,2,1,0:T(8,128)S(1)} %get-tuple-element.310), channel_id=1, source_target_pairs={{4,0},{8,4},{12,8},{16,12},{20,16},{24,20},{28,24},{5,1},{9,5},{13... | collective-permute-start | bytes 393224 | tf_op jit(solution)/shard_map/ppermute | solution.py:30
  138.1 6.9 %collective-permute-start.15 = (f32[8,1,8,512]{3,2,1,0:T(8,128)S(1)}, f32[8,1,8,512]{3,2,1,0:T(8,128)S(1)}, u32[]{:S(2)}, u32[]{:S(2)}) collective-permute-start(f32[8,1,8,512]{3,2,1,0:T(8,128)S(1)} %get-tuple-element.309), channel_id=1, source_target_pairs={{0,4},{4,8},{8,12},{12,16},{16,20},{20,24},{24,28},{1,5},{5,9},{9,... | collective-permute-start | bytes 393224 | tf_op jit(solution)/shard_map/ppermute | solution.py:28
  145.1 4.5 %collective-permute-start.16 = (f32[8,4,1,512]{3,2,1,0:T(1,128)S(1)}, f32[8,4,1,512]{3,2,1,0:T(1,128)S(1)}, u32[]{:S(2)}, u32[]{:S(2)}) collective-permute-start(f32[8,4,1,512]{3,2,1,0:T(1,128)S(1)} %get-tuple-element.280), channel_id=1, source_target_pairs={{1,0},{2,1},{3,2},{5,4},{6,5},{7,6},{9,8},{10,9},{11,10},{13,12},{... | collective-permute-start | bytes 196616 | tf_op jit(solution)/shard_map/ppermute | solution.py:30
  147.0 5.6 %collective-permute-start.17 = (f32[8,4,1,512]{3,2,1,0:T(1,128)S(1)}, f32[8,4,1,512]{3,2,1,0:T(1,128)S(1)}, u32[]{:S(2)}, u32[]{:S(2)}) collective-permute-start(f32[8,4,1,512]{3,2,1,0:T(1,128)S(1)} %get-tuple-element.281), channel_id=1, source_target_pairs={{0,1},{1,2},{2,3},{4,5},{5,6},{6,7},{8,9},{9,10},{10,11},{12,13},{... | collective-permute-start | bytes 196616 | tf_op jit(solution)/shard_map/ppermute | solution.py:28
  152.9 7.8 %collective-permute-start.18 = (f32[8,1,8,512]{3,2,1,0:T(8,128)S(1)}, f32[8,1,8,512]{3,2,1,0:T(8,128)S(1)}, u32[]{:S(2)}, u32[]{:S(2)}) collective-permute-start(f32[8,1,8,512]{3,2,1,0:T(8,128)S(1)} %get-tuple-element.306), channel_id=1, source_target_pairs={{4,0},{8,4},{12,8},{16,12},{20,16},{24,20},{28,24},{5,1},{9,5},{13... | collective-permute-start | bytes 393224 | tf_op jit(solution)/shard_map/ppermute | solution.py:30
  154.8 7.3 %collective-permute-start.19 = (f32[8,1,8,512]{3,2,1,0:T(8,128)S(1)}, f32[8,1,8,512]{3,2,1,0:T(8,128)S(1)}, u32[]{:S(2)}, u32[]{:S(2)}) collective-permute-start(f32[8,1,8,512]{3,2,1,0:T(8,128)S(1)} %get-tuple-element.305), channel_id=1, source_target_pairs={{0,4},{4,8},{8,12},{12,16},{16,20},{20,24},{24,28},{1,5},{5,9},{9,... | collective-permute-start | bytes 393224 | tf_op jit(solution)/shard_map/ppermute | solution.py:28
  164.2 5.6 %collective-permute-start.21 = (f32[8,4,1,512]{3,2,1,0:T(1,128)S(1)}, f32[8,4,1,512]{3,2,1,0:T(1,128)S(1)}, u32[]{:S(2)}, u32[]{:S(2)}) collective-permute-start(f32[8,4,1,512]{3,2,1,0:T(1,128)S(1)} %get-tuple-element.279), channel_id=1, source_target_pairs={{0,1},{1,2},{2,3},{4,5},{5,6},{6,7},{8,9},{9,10},{10,11},{12,13},{... | collective-permute-start | bytes 196616 | tf_op jit(solution)/shard_map/ppermute | solution.py:28
  170.1 8.3 %collective-permute-start.22 = (f32[8,1,8,512]{3,2,1,0:T(8,128)S(1)}, f32[8,1,8,512]{3,2,1,0:T(8,128)S(1)}, u32[]{:S(2)}, u32[]{:S(2)}) collective-permute-start(f32[8,1,8,512]{3,2,1,0:T(8,128)S(1)} %get-tuple-element.302), channel_id=1, source_target_pairs={{4,0},{8,4},{12,8},{16,12},{20,16},{24,20},{28,24},{5,1},{9,5},{13... | collective-permute-start | bytes 393224 | tf_op jit(solution)/shard_map/ppermute | solution.py:30
  172.0 7.8 %collective-permute-start.23 = (f32[8,1,8,512]{3,2,1,0:T(8,128)S(1)}, f32[8,1,8,512]{3,2,1,0:T(8,128)S(1)}, u32[]{:S(2)}, u32[]{:S(2)}) collective-permute-start(f32[8,1,8,512]{3,2,1,0:T(8,128)S(1)} %get-tuple-element.301), channel_id=1, source_target_pairs={{0,4},{4,8},{8,12},{12,16},{16,20},{20,24},{24,28},{1,5},{5,9},{9,... | collective-permute-start | bytes 393224 | tf_op jit(solution)/shard_map/ppermute | solution.py:28
  179.9 4.5 %collective-permute-start.24 = (f32[8,4,1,512]{3,2,1,0:T(1,128)S(1)}, f32[8,4,1,512]{3,2,1,0:T(1,128)S(1)}, u32[]{:S(2)}, u32[]{:S(2)}) collective-permute-start(f32[8,4,1,512]{3,2,1,0:T(1,128)S(1)} %get-tuple-element.276), channel_id=1, source_target_pairs={{1,0},{2,1},{3,2},{5,4},{6,5},{7,6},{9,8},{10,9},{11,10},{13,12},{... | collective-permute-start | bytes 196616 | tf_op jit(solution)/shard_map/ppermute | solution.py:30
  181.9 5.6 %collective-permute-start.25 = (f32[8,4,1,512]{3,2,1,0:T(1,128)S(1)}, f32[8,4,1,512]{3,2,1,0:T(1,128)S(1)}, u32[]{:S(2)}, u32[]{:S(2)}) collective-permute-start(f32[8,4,1,512]{3,2,1,0:T(1,128)S(1)} %get-tuple-element.277), channel_id=1, source_target_pairs={{0,1},{1,2},{2,3},{4,5},{5,6},{6,7},{8,9},{9,10},{10,11},{12,13},{... | collective-permute-start | bytes 196616 | tf_op jit(solution)/shard_map/ppermute | solution.py:28
  187.8 8.2 %collective-permute-start.26 = (f32[8,1,8,512]{3,2,1,0:T(8,128)S(1)}, f32[8,1,8,512]{3,2,1,0:T(8,128)S(1)}, u32[]{:S(2)}, u32[]{:S(2)}) collective-permute-start(f32[8,1,8,512]{3,2,1,0:T(8,128)S(1)} %get-tuple-element.298), channel_id=1, source_target_pairs={{4,0},{8,4},{12,8},{16,12},{20,16},{24,20},{28,24},{5,1},{9,5},{13... | collective-permute-start | bytes 393224 | tf_op jit(solution)/shard_map/ppermute | solution.py:30
  189.7 7.8 %collective-permute-start.27 = (f32[8,1,8,512]{3,2,1,0:T(8,128)S(1)}, f32[8,1,8,512]{3,2,1,0:T(8,128)S(1)}, u32[]{:S(2)}, u32[]{:S(2)}) collective-permute-start(f32[8,1,8,512]{3,2,1,0:T(8,128)S(1)} %get-tuple-element.297), channel_id=1, source_target_pairs={{0,4},{4,8},{8,12},{12,16},{16,20},{20,24},{24,28},{1,5},{5,9},{9,... | collective-permute-start | bytes 393224 | tf_op jit(solution)/shard_map/ppermute | solution.py:28
  197.5 4.5 %collective-permute-start.28 = (f32[8,4,1,512]{3,2,1,0:T(1,128)S(1)}, f32[8,4,1,512]{3,2,1,0:T(1,128)S(1)}, u32[]{:S(2)}, u32[]{:S(2)}) collective-permute-start(f32[8,4,1,512]{3,2,1,0:T(1,128)S(1)} %get-tuple-element.274), channel_id=1, source_target_pairs={{1,0},{2,1},{3,2},{5,4},{6,5},{7,6},{9,8},{10,9},{11,10},{13,12},{... | collective-permute-start | bytes 196616 | tf_op jit(solution)/shard_map/ppermute | solution.py:30
  199.5 5.6 %collective-permute-start.29 = (f32[8,4,1,512]{3,2,1,0:T(1,128)S(1)}, f32[8,4,1,512]{3,2,1,0:T(1,128)S(1)}, u32[]{:S(2)}, u32[]{:S(2)}) collective-permute-start(f32[8,4,1,512]{3,2,1,0:T(1,128)S(1)} %get-tuple-element.275), channel_id=1, source_target_pairs={{0,1},{1,2},{2,3},{4,5},{5,6},{6,7},{8,9},{9,10},{10,11},{12,13},{... | collective-permute-start | bytes 196616 | tf_op jit(solution)/shard_map/ppermute | solution.py:28
  276.8 7.8 %collective-permute-start.30 = (f32[8,1,8,512]{3,2,1,0:T(8,128)S(1)}, f32[8,1,8,512]{3,2,1,0:T(8,128)S(1)}, u32[]{:S(2)}, u32[]{:S(2)}) collective-permute-start(f32[8,1,8,512]{3,2,1,0:T(8,128)S(1)} %get-tuple-element.294), channel_id=1, source_target_pairs={{4,0},{8,4},{12,8},{16,12},{20,16},{24,20},{28,24},{5,1},{9,5},{13... | collective-permute-start | bytes 393224 | tf_op jit(solution)/shard_map/ppermute | solution.py:30
  281.4 6.9 %collective-permute-start.31 = (f32[8,1,8,512]{3,2,1,0:T(8,128)S(1)}, f32[8,1,8,512]{3,2,1,0:T(8,128)S(1)}, u32[]{:S(2)}, u32[]{:S(2)}) collective-permute-start(f32[8,1,8,512]{3,2,1,0:T(8,128)S(1)} %get-tuple-element.293), channel_id=1, source_target_pairs={{0,4},{4,8},{8,12},{12,16},{16,20},{20,24},{24,28},{1,5},{5,9},{9,... | collective-permute-start | bytes 393224 | tf_op jit(solution)/shard_map/ppermute | solution.py:28
  290.3 5.6 %collective-permute-start.33 = (f32[8,4,1,512]{3,2,1,0:T(1,128)S(1)}, f32[8,4,1,512]{3,2,1,0:T(1,128)S(1)}, u32[]{:S(2)}, u32[]{:S(2)}) collective-permute-start(f32[8,4,1,512]{3,2,1,0:T(1,128)S(1)} %get-tuple-element.273), channel_id=1, source_target_pairs={{0,1},{1,2},{2,3},{4,5},{5,6},{6,7},{8,9},{9,10},{10,11},{12,13},{... | collective-permute-start | bytes 196616 | tf_op jit(solution)/shard_map/ppermute | solution.py:28
  (3 other events, 22.8 us)
where the time goes:
time: 298 us; the launch traced here: 297 us
  starting transfers between devices  95.1 us (32%)
  local copies, waits for them, and re-layouts  66.9 us (22%)
  blocking collectives  61.9 us (21%)
  waiting for transfers between devices  46.4 us (16%)
  other arithmetic  19.8 us (7%)
  matrix products  5.65 us (2%)
    all_gather x2, blocking collectives, per_device(): gathered = lax.all_gather(first, 'slab', axis=1, tiled=True)  61.9 us
    gather x2, local copies, waits for them, and re-layouts, per_device(): correction = jnp.take(second, flat_ids, axis=1).reshape(LABELS, CZ, CY, NX)  55.7 us
    ppermute x16, starting transfers between devices, padded(): lax.ppermute(tail, axis, [(i, (i + 1) % count) for i in range(ends)])  52.2 us
    ppermute x16, waiting for transfers between devices, padded(): lax.ppermute(tail, axis, [(i, (i + 1) % count) for i in range(ends)])  39 us
    ppermute x16, starting transfers between devices, padded(): lax.ppermute(head, axis, [((i + 1) % count, i) for i in range(ends)])  38.5 us
    select_n x2, other arithmetic, per_device(): correction = jnp.take(second, flat_ids, axis=1).reshape(LABELS, CZ, CY, NX)  14.9 us
    ppermute x16, waiting for transfers between devices, padded(): lax.ppermute(head, axis, [((i + 1) % count, i) for i in range(ends)])  7.38 us
  transfers between devices with their start and end apart: 34, of which 22 were waited for; matrix products, arithmetic and copies ran while one was open for 2% of the time, Pallas kernels for 0%

commit v1 on v0

--- a/solution.py
+++ b/solution.py
@@ -15,6 +15,12 @@
 smooth_step = 0.8
 coarse_step = 0.7
 weight_unit = 0.125
+
+
+def in_order(pieces, dim):
+    shape = list(pieces.shape[1:])
+    shape[dim] *= pieces.shape[0]
+    return jnp.moveaxis(pieces, 0, dim).reshape(shape)
 
 
 def padded(cells, sides, width):
@@ -140,7 +146,19 @@
             0, cells // span, collect_block, jnp.zeros((LABELS, CC), jnp.float32)
         )
         first = coarse_step * coarse_rhs / coarse_diag
-        gathered = lax.all_gather(first, "slab", axis=1, tiled=True)
+        size = lax.axis_size("slab")
+        pairs = [(i_2, (i_2 + 1) % size) for i_2 in range(size)]
+        back = [(b, a_2) for a_2, b in pairs]
+        lower, upper = ([], [])
+        for step in range(size - 1):
+            if step % 2 == 0:
+                lower.append(lax.ppermute(lower[-1] if lower else first, "slab", pairs))
+            else:
+                upper.append(lax.ppermute(upper[-1] if upper else first, "slab", back))
+        blocks = jnp.stack([*lower[::-1], first, *upper])
+        shift = lax.axis_index("slab") - len(lower)
+        blocks = blocks[(jnp.arange(size) - shift) % size]
+        gathered = in_order(blocks, 1)
         arranged = gathered.reshape(LABELS, group, sections, CC)
         section = lax.dynamic_slice_in_dim(arranged, section_id, 1, 2).reshape(LABELS, group * CC)
         second = (

time: 298 us -> 283 us (0.950)
  blocking collectives: 61.9 us -> 0 us
  starting transfers between devices: 95.1 us -> 127 us
  waiting for transfers between devices: 46.4 us -> 60.7 us
    all_gather x2 -> x0, blocking collectives: 61.9 us -> none  [per_device(): gathered = lax.all_gather(first, 'slab', axis=1, tiled=True)]
    ppermute x0 -> x14, starting transfers between devices: none -> 30.5 us  [the longest x8 23.8 us: per_device(): lower.append(lax.ppermute(lower[-1] if lower else first, 'slab', pairs))]
    ppermute x0 -> x14, waiting for transfers between devices: none -> 12.6 us  [the longest x8 11.3 us: per_device(): lower.append(lax.ppermute(lower[-1] if lower else first, 'slab', pairs))]
  transfers between devices with their start and end apart: 34 -> 48, of which waited for: 22 -> 33; matrix products, arithmetic and copies ran while one was open for 2% -> 2% of each run, Pallas kernels for 0% -> 0%
where the time goes in v1:
time: 283 us; the launch traced here: 281 us
  starting transfers between devices  127 us (45%)
  local copies, waits for them, and re-layouts  67.1 us (24%)
  waiting for transfers between devices  60.7 us (21%)
  other arithmetic  19.9 us (7%)
  matrix products  5.66 us (2%)
    gather x2, local copies, waits for them, and re-layouts, per_device(): correction = jnp.take(second, flat_ids, axis=1).reshape(LABELS, CZ, CY, NX)  55.5 us
    ppermute x16, starting transfers between devices, padded(): lax.ppermute(tail, axis, [(i, (i + 1) % count) for i in range(ends)])  50.9 us
    ppermute x16, starting transfers between devices, padded(): lax.ppermute(head, axis, [((i + 1) % count, i) for i in range(ends)])  41 us
    ppermute x16, waiting for transfers between devices, padded(): lax.ppermute(tail, axis, [(i, (i + 1) % count) for i in range(ends)])  40.8 us
    ppermute x8, starting transfers between devices, per_device(): lower.append(lax.ppermute(lower[-1] if lower else first, 'slab', pairs))  23.8 us
    select_n x2, other arithmetic, per_device(): correction = jnp.take(second, flat_ids, axis=1).reshape(LABELS, CZ, CY, NX)  14.9 us
    ppermute x8, waiting for transfers between devices, per_device(): lower.append(lax.ppermute(lower[-1] if lower else first, 'slab', pairs))  11.3 us
    ppermute x6, starting transfers between devices, per_device(): upper.append(lax.ppermute(upper[-1] if upper else first, 'slab', back))  6.68 us
  transfers between devices with their start and end apart: 48, of which 33 were waited for; matrix products, arithmetic and copies ran while one was open for 2% of the time, Pallas kernels for 0%

profile of v1, /device:TPU:6, one launch (start us, length us, event | category | flops | bytes accessed | tf_op | source)
XLA Modules:
  0.0 281.3 jit_solution(2108593669914386730)
XLA Ops:
  2.6 4.3 %collective-permute-start.3 = (f32[8,1,8,512]{3,2,1,0:T(8,128)S(1)}, f32[8,1,8,512]{3,2,1,0:T(8,128)S(1)}, u32[]{:S(2)}, u32[]{:S(2)}) collective-permute-start(f32[8,1,8,512]{3,2,1,0:T(8,128)S(1)} %broadcast.209), channel_id=1, source_target_pairs={{0,4},{4,8},{8,12},{12,16},{16,20},{20,24},{24,28},{1,5},{5,9},{9,... | collective-permute-start | bytes 393224 | tf_op jit(solution)/shard_map/ppermute | solution.py:34
  20.8 3.1 %collective-permute-done.5 = f32[8,4,1,512]{3,2,1,0:T(1,128)S(1)} collective-permute-done((f32[8,4,1,512]{3,2,1,0:T(1,128)S(1)}, f32[8,4,1,512]{3,2,1,0:T(1,128)S(1)}, u32[]{:S(2)}, u32[]{:S(2)}) %collective-permute-start.5) | collective-permute-done | bytes 65568 | tf_op jit(solution)/shard_map/ppermute | solution.py:34
  24.2 3.3 %collective-permute-start.6 = (f32[8,1,8,512]{3,2,1,0:T(8,128)S(1)}, f32[8,1,8,512]{3,2,1,0:T(8,128)S(1)}, u32[]{:S(2)}, u32[]{:S(2)}) collective-permute-start(f32[8,1,8,512]{3,2,1,0:T(8,128)S(1)} %get-tuple-element.318), channel_id=1, source_target_pairs={{4,0},{8,4},{12,8},{16,12},{20,16},{24,20},{28,24},{5,1},{9,5},{13... | collective-permute-start | bytes 393224 | tf_op jit(solution)/shard_map/ppermute | solution.py:36
  27.4 3.5 %collective-permute-start.7 = (f32[8,1,8,512]{3,2,1,0:T(8,128)S(1)}, f32[8,1,8,512]{3,2,1,0:T(8,128)S(1)}, u32[]{:S(2)}, u32[]{:S(2)}) collective-permute-start(f32[8,1,8,512]{3,2,1,0:T(8,128)S(1)} %get-tuple-element.317), channel_id=1, source_target_pairs={{0,4},{4,8},{8,12},{12,16},{16,20},{20,24},{24,28},{1,5},{5,9},{9,... | collective-permute-start | bytes 393224 | tf_op jit(solution)/shard_map/ppermute | solution.py:34
  38.9 3.0 %collective-permute-done.9 = f32[8,4,1,512]{3,2,1,0:T(1,128)S(1)} collective-permute-done((f32[8,4,1,512]{3,2,1,0:T(1,128)S(1)}, f32[8,4,1,512]{3,2,1,0:T(1,128)S(1)}, u32[]{:S(2)}, u32[]{:S(2)}) %collective-permute-start.9) | collective-permute-done | bytes 65568 | tf_op jit(solution)/shard_map/ppermute | solution.py:34
  44.1 4.8 %collective-permute-start.11 = (f32[8,1,8,512]{3,2,1,0:T(8,128)S(1)}, f32[8,1,8,512]{3,2,1,0:T(8,128)S(1)}, u32[]{:S(2)}, u32[]{:S(2)}) collective-permute-start(f32[8,1,8,512]{3,2,1,0:T(8,128)S(1)} %get-tuple-element.313), channel_id=1, source_target_pairs={{0,4},{4,8},{8,12},{12,16},{16,20},{20,24},{24,28},{1,5},{5,9},{9,... | collective-permute-start | bytes 393224 | tf_op jit(solution)/shard_map/ppermute | solution.py:34
  56.1 3.0 %collective-permute-done.13 = f32[8,4,1,512]{3,2,1,0:T(1,128)S(1)} collective-permute-done((f32[8,4,1,512]{3,2,1,0:T(1,128)S(1)}, f32[8,4,1,512]{3,2,1,0:T(1,128)S(1)}, u32[]{:S(2)}, u32[]{:S(2)}) %collective-permute-start.13) | collective-permute-done | bytes 65568 | tf_op jit(solution)/shard_map/ppermute | solution.py:34
  62.0 3.4 %collective-permute-start.14 = (f32[8,128]{1,0:T(8,128)S(1)}, f32[8,128]{1,0:T(8,128)S(1)}, u32[]{:S(2)}, u32[]{:S(2)}) collective-permute-start(f32[8,128]{1,0:T(8,128)S(1)} %multiply_divide_fusion.1), channel_id=1, source_target_pairs={{0,4},{4,8},{8,12},{12,16},{16,20},{20,24},{24,28},{28,0},{1,5},{5... | collective-permute-start | bytes 12296 | tf_op jit(solution)/shard_map/ppermute | solution.py:155
  66.7 3.2 %collective-permute-start.15 = (f32[8,128]{1,0:T(8,128)S(1)}, f32[8,128]{1,0:T(8,128)S(1)}, u32[]{:S(2)}, u32[]{:S(2)}) collective-permute-start(f32[8,128]{1,0:T(8,128)S(1)} %collective-permute-done.14), channel_id=1, source_target_pairs={{0,4},{4,8},{8,12},{12,16},{16,20},{20,24},{24,28},{28,0},{1,5},{5... | collective-permute-start | bytes 12296 | tf_op jit(solution)/shard_map/ppermute | solution.py:155
  71.3 3.2 %collective-permute-start.16 = (f32[8,128]{1,0:T(8,128)S(1)}, f32[8,128]{1,0:T(8,128)S(1)}, u32[]{:S(2)}, u32[]{:S(2)}) collective-permute-start(f32[8,128]{1,0:T(8,128)S(1)} %collective-permute-done.15), channel_id=1, source_target_pairs={{0,4},{4,8},{8,12},{12,16},{16,20},{20,24},{24,28},{28,0},{1,5},{5... | collective-permute-start | bytes 12296 | tf_op jit(solution)/shard_map/ppermute | solution.py:155
  79.0 3.4 %collective-permute-start.20 = (f32[8,128]{1,0:T(8,128)S(1)}, f32[8,128]{1,0:T(8,128)S(1)}, u32[]{:S(2)}, u32[]{:S(2)}) collective-permute-start(f32[8,128]{1,0:T(8,128)S(1)} %collective-permute-done.19), channel_id=1, source_target_pairs={{4,0},{8,4},{12,8},{16,12},{20,16},{24,20},{28,24},{0,28},{5,1},{9... | collective-permute-start | bytes 12296 | tf_op jit(solution)/shard_map/ppermute | solution.py:157
  85.1 27.8 %gather_fusion.3 = f32[8192,8]{1,0:T(8,128)} fusion(f32[8,128]{0,1:T(8,128)S(1)} %copy.9, s32[8192]{0:T(1024)S(1)} %fusion.124), kind=kCustom, calls=%fused_computation.clone | custom fusion | bytes 557056 | tf_op jit(solution)/shard_map/jit(_take)/gather | solution.py:179
  112.9 7.5 %broadcast_select_fusion.1 = f32[8192,8]{1,0:T(8,128)} fusion(f32[8192,8]{1,0:T(8,128)} %gather_fusion.3, pred[8192]{0:T(1024)(128)(4,1)S(1)} %compare_and_fusion), kind=kLoop, calls=%fused_computation.18 | loop fusion | flops 65536 | bytes 532480 | tf_op jit(solution)/shard_map/jit(_take)/select_n | solution.py:179
  120.3 2.8 %copy.10 = f32[8,2,8,512]{3,2,1,0:T(8,128)S(1)} copy(f32[8,2,8,512]{0,3,2,1:T(8,128)} %bitcast.91) | data formatting | bytes 524288 | tf_op jit(solution)/shard_map/reshape | solution.py:179
  123.3 6.6 %collective-permute-start.21 = (f32[8,1,8,512]{3,2,1,0:T(8,128)S(1)}, f32[8,1,8,512]{3,2,1,0:T(8,128)S(1)}, u32[]{:S(2)}, u32[]{:S(2)}) collective-permute-start(f32[8,1,8,512]{3,2,1,0:T(8,128)S(1)} %get-tuple-element.310), channel_id=1, source_target_pairs={{4,0},{8,4},{12,8},{16,12},{20,16},{24,20},{28,24},{5,1},{9,5},{13... | collective-permute-start | bytes 393224 | tf_op jit(solution)/shard_map/ppermute | solution.py:36
  132.4 4.4 %collective-permute-done.22 = f32[8,1,8,512]{3,2,1,0:T(8,128)S(1)} collective-permute-done((f32[8,1,8,512]{3,2,1,0:T(8,128)S(1)}, f32[8,1,8,512]{3,2,1,0:T(8,128)S(1)}, u32[]{:S(2)}, u32[]{:S(2)}) %collective-permute-start.22) | collective-permute-done | bytes 131104 | tf_op jit(solution)/shard_map/ppermute | solution.py:34
  141.3 3.0 %collective-permute-done.24 = f32[8,4,1,512]{3,2,1,0:T(1,128)S(1)} collective-permute-done((f32[8,4,1,512]{3,2,1,0:T(1,128)S(1)}, f32[8,4,1,512]{3,2,1,0:T(1,128)S(1)}, u32[]{:S(2)}, u32[]{:S(2)}) %collective-permute-start.24) | collective-permute-done | bytes 65568 | tf_op jit(solution)/shard_map/ppermute | solution.py:34
  146.6 4.8 %collective-permute-start.26 = (f32[8,1,8,512]{3,2,1,0:T(8,128)S(1)}, f32[8,1,8,512]{3,2,1,0:T(8,128)S(1)}, u32[]{:S(2)}, u32[]{:S(2)}) collective-permute-start(f32[8,1,8,512]{3,2,1,0:T(8,128)S(1)} %get-tuple-element.305), channel_id=1, source_target_pairs={{0,4},{4,8},{8,12},{12,16},{16,20},{20,24},{24,28},{1,5},{5,9},{9,... | collective-permute-start | bytes 393224 | tf_op jit(solution)/shard_map/ppermute | solution.py:34
  158.5 3.0 %collective-permute-done.28 = f32[8,4,1,512]{3,2,1,0:T(1,128)S(1)} collective-permute-done((f32[8,4,1,512]{3,2,1,0:T(1,128)S(1)}, f32[8,4,1,512]{3,2,1,0:T(1,128)S(1)}, u32[]{:S(2)}, u32[]{:S(2)}) %collective-permute-start.28) | collective-permute-done | bytes 65568 | tf_op jit(solution)/shard_map/ppermute | solution.py:34
  163.8 5.3 %collective-permute-start.30 = (f32[8,1,8,512]{3,2,1,0:T(8,128)S(1)}, f32[8,1,8,512]{3,2,1,0:T(8,128)S(1)}, u32[]{:S(2)}, u32[]{:S(2)}) collective-permute-start(f32[8,1,8,512]{3,2,1,0:T(8,128)S(1)} %get-tuple-element.301), channel_id=1, source_target_pairs={{0,4},{4,8},{8,12},{12,16},{16,20},{20,24},{24,28},{1,5},{5,9},{9,... | collective-permute-start | bytes 393224 | tf_op jit(solution)/shard_map/ppermute | solution.py:34
  176.2 3.0 %collective-permute-done.32 = f32[8,4,1,512]{3,2,1,0:T(1,128)S(1)} collective-permute-done((f32[8,4,1,512]{3,2,1,0:T(1,128)S(1)}, f32[8,4,1,512]{3,2,1,0:T(1,128)S(1)}, u32[]{:S(2)}, u32[]{:S(2)}) %collective-permute-start.32) | collective-permute-done | bytes 65568 | tf_op jit(solution)/shard_map/ppermute | solution.py:34
  181.5 5.2 %collective-permute-start.34 = (f32[8,1,8,512]{3,2,1,0:T(8,128)S(1)}, f32[8,1,8,512]{3,2,1,0:T(8,128)S(1)}, u32[]{:S(2)}, u32[]{:S(2)}) collective-permute-start(f32[8,1,8,512]{3,2,1,0:T(8,128)S(1)} %get-tuple-element.297), channel_id=1, source_target_pairs={{0,4},{4,8},{8,12},{12,16},{16,20},{20,24},{24,28},{1,5},{5,9},{9,... | collective-permute-start | bytes 393224 | tf_op jit(solution)/shard_map/ppermute | solution.py:34
  193.8 3.0 %collective-permute-done.36 = f32[8,4,1,512]{3,2,1,0:T(1,128)S(1)} collective-permute-done((f32[8,4,1,512]{3,2,1,0:T(1,128)S(1)}, f32[8,4,1,512]{3,2,1,0:T(1,128)S(1)}, u32[]{:S(2)}, u32[]{:S(2)}) %collective-permute-start.36) | collective-permute-done | bytes 65568 | tf_op jit(solution)/shard_map/ppermute | solution.py:34
  199.7 3.3 %collective-permute-start.37 = (f32[8,128]{1,0:T(8,128)S(1)}, f32[8,128]{1,0:T(8,128)S(1)}, u32[]{:S(2)}, u32[]{:S(2)}) collective-permute-start(f32[8,128]{1,0:T(8,128)S(1)} %multiply_divide_fusion), channel_id=1, source_target_pairs={{0,4},{4,8},{8,12},{12,16},{16,20},{20,24},{24,28},{28,0},{1,5},{5... | collective-permute-start | bytes 12296 | tf_op jit(solution)/shard_map/ppermute | solution.py:155
  204.4 3.2 %collective-permute-start.38 = (f32[8,128]{1,0:T(8,128)S(1)}, f32[8,128]{1,0:T(8,128)S(1)}, u32[]{:S(2)}, u32[]{:S(2)}) collective-permute-start(f32[8,128]{1,0:T(8,128)S(1)} %collective-permute-done.37), channel_id=1, source_target_pairs={{0,4},{4,8},{8,12},{12,16},{16,20},{20,24},{24,28},{28,0},{1,5},{5... | collective-permute-start | bytes 12296 | tf_op jit(solution)/shard_map/ppermute | solution.py:155
  208.9 3.2 %collective-permute-start.39 = (f32[8,128]{1,0:T(8,128)S(1)}, f32[8,128]{1,0:T(8,128)S(1)}, u32[]{:S(2)}, u32[]{:S(2)}) collective-permute-start(f32[8,128]{1,0:T(8,128)S(1)} %collective-permute-done.38), channel_id=1, source_target_pairs={{0,4},{4,8},{8,12},{12,16},{16,20},{20,24},{24,28},{28,0},{1,5},{5... | collective-permute-start | bytes 12296 | tf_op jit(solution)/shard_map/ppermute | solution.py:155
  213.5 3.0 %collective-permute-start.40 = (f32[8,128]{1,0:T(8,128)S(1)}, f32[8,128]{1,0:T(8,128)S(1)}, u32[]{:S(2)}, u32[]{:S(2)}) collective-permute-start(f32[8,128]{1,0:T(8,128)S(1)} %collective-permute-done.39), channel_id=1, source_target_pairs={{0,4},{4,8},{8,12},{12,16},{16,20},{20,24},{24,28},{28,0},{1,5},{5... | collective-permute-start | bytes 12296 | tf_op jit(solution)/shard_map/ppermute | solution.py:155
  222.3 27.8 %gather_fusion.4 = f32[8192,8]{1,0:T(8,128)} fusion(f32[8,128]{0,1:T(8,128)S(1)} %copy.11, s32[8192]{0:T(1024)S(1)} %fusion.124), kind=kCustom, calls=%fused_computation.1.clone | custom fusion | bytes 557056 | tf_op jit(solution)/shard_map/jit(_take)/gather | solution.py:179
  250.0 7.5 %broadcast_select_fusion = f32[8192,8]{1,0:T(8,128)} fusion(f32[8192,8]{1,0:T(8,128)} %gather_fusion.4, pred[8192]{0:T(1024)(128)(4,1)S(1)} %compare_and_fusion), kind=kLoop, calls=%fused_computation.17 | loop fusion | flops 65536 | bytes 532480 | tf_op jit(solution)/shard_map/jit(_take)/select_n | solution.py:179
  260.4 5.4 %collective-permute-start.44 = (f32[8,1,8,512]{3,2,1,0:T(8,128)S(1)}, f32[8,1,8,512]{3,2,1,0:T(8,128)S(1)}, u32[]{:S(2)}, u32[]{:S(2)}) collective-permute-start(f32[8,1,8,512]{3,2,1,0:T(8,128)S(1)} %get-tuple-element.294), channel_id=1, source_target_pairs={{4,0},{8,4},{12,8},{16,12},{20,16},{24,20},{28,24},{5,1},{9,5},{13... | collective-permute-start | bytes 393224 | tf_op jit(solution)/shard_map/ppermute | solution.py:36
  268.4 4.4 %collective-permute-done.45 = f32[8,1,8,512]{3,2,1,0:T(8,128)S(1)} collective-permute-done((f32[8,1,8,512]{3,2,1,0:T(8,128)S(1)}, f32[8,1,8,512]{3,2,1,0:T(8,128)S(1)}, u32[]{:S(2)}, u32[]{:S(2)}) %collective-permute-start.45) | collective-permute-done | bytes 131104 | tf_op jit(solution)/shard_map/ppermute | solution.py:34
  277.3 3.0 %collective-permute-done.47 = f32[8,4,1,512]{3,2,1,0:T(1,128)S(1)} collective-permute-done((f32[8,4,1,512]{3,2,1,0:T(1,128)S(1)}, f32[8,4,1,512]{3,2,1,0:T(1,128)S(1)}, u32[]{:S(2)}, u32[]{:S(2)}) %collective-permute-start.47) | collective-permute-done | bytes 65568 | tf_op jit(solution)/shard_map/ppermute | solution.py:34
  (179 shorter events, 109.9 us)
Async XLA Ops:
  0.0 16.2 %collective-permute-start.2 = (f32[8,1,8,512]{3,2,1,0:T(8,128)S(1)}, f32[8,1,8,512]{3,2,1,0:T(8,128)S(1)}, u32[]{:S(2)}, u32[]{:S(2)}) collective-permute-start(f32[8,1,8,512]{3,2,1,0:T(8,128)S(1)} %broadcast.209), channel_id=1, source_target_pairs={{4,0},{8,4},{12,8},{16,12},{20,16},{24,20},{28,24},{5,1},{9,5},{13... | collective-permute-start | bytes 393224 | tf_op jit(solution)/shard_map/ppermute | solution.py:36
  2.6 13.6 %collective-permute-start.3 = (f32[8,1,8,512]{3,2,1,0:T(8,128)S(1)}, f32[8,1,8,512]{3,2,1,0:T(8,128)S(1)}, u32[]{:S(2)}, u32[]{:S(2)}) collective-permute-start(f32[8,1,8,512]{3,2,1,0:T(8,128)S(1)} %broadcast.209), channel_id=1, source_target_pairs={{0,4},{4,8},{8,12},{12,16},{16,20},{20,24},{24,28},{1,5},{5,9},{9,... | collective-permute-start | bytes 393224 | tf_op jit(solution)/shard_map/ppermute | solution.py:34
  7.6 6.3 %collective-permute-start = (s32[1,8,512]{2,1,0:T(8,128)S(1)}, s32[1,8,512]{2,1,0:T(8,128)S(1)}, u32[]{:S(2)}, u32[]{:S(2)}) collective-permute-start(s32[1,8,512]{2,1,0:T(8,128)S(1)} %slice_bitcast_fusion.4), channel_id=1, source_target_pairs={{0,4},{4,8},{8,12},{12,16},{16,20},{20,24},{24,28},{1,5},{5,9},{9,... | collective-permute-start | bytes 49160 | tf_op jit(solution)/shard_map/ppermute | solution.py:46
  10.9 4.9 %collective-permute-start.1 = (s32[2,1,512]{2,1,0:T(1,128)S(1)}, s32[2,1,512]{2,1,0:T(1,128)S(1)}, u32[]{:S(2)}, u32[]{:S(2)}) collective-permute-start(s32[2,1,512]{2,1,0:T(1,128)S(1)} %slice_bitcast_fusion.5), channel_id=1, source_target_pairs={{0,1},{1,2},{2,3},{4,5},{5,6},{6,7},{8,9},{9,10},{10,11},{12,13},{... | collective-permute-start | bytes 12296 | tf_op jit(solution)/shard_map/ppermute | solution.py:46
  18.3 5.6 %collective-permute-start.5 = (f32[8,4,1,512]{3,2,1,0:T(1,128)S(1)}, f32[8,4,1,512]{3,2,1,0:T(1,128)S(1)}, u32[]{:S(2)}, u32[]{:S(2)}) collective-permute-start(f32[8,4,1,512]{3,2,1,0:T(1,128)S(1)} %get-tuple-element.287), channel_id=1, source_target_pairs={{0,1},{1,2},{2,3},{4,5},{5,6},{6,7},{8,9},{9,10},{10,11},{12,13},{... | collective-permute-start | bytes 196616 | tf_op jit(solution)/shard_map/ppermute | solution.py:34
  24.2 7.9 %collective-permute-start.6 = (f32[8,1,8,512]{3,2,1,0:T(8,128)S(1)}, f32[8,1,8,512]{3,2,1,0:T(8,128)S(1)}, u32[]{:S(2)}, u32[]{:S(2)}) collective-permute-start(f32[8,1,8,512]{3,2,1,0:T(8,128)S(1)} %get-tuple-element.318), channel_id=1, source_target_pairs={{4,0},{8,4},{12,8},{16,12},{20,16},{24,20},{28,24},{5,1},{9,5},{13... | collective-permute-start | bytes 393224 | tf_op jit(solution)/shard_map/ppermute | solution.py:36
  27.4 6.9 %collective-permute-start.7 = (f32[8,1,8,512]{3,2,1,0:T(8,128)S(1)}, f32[8,1,8,512]{3,2,1,0:T(8,128)S(1)}, u32[]{:S(2)}, u32[]{:S(2)}) collective-permute-start(f32[8,1,8,512]{3,2,1,0:T(8,128)S(1)} %get-tuple-element.317), channel_id=1, source_target_pairs={{0,4},{4,8},{8,12},{12,16},{16,20},{20,24},{24,28},{1,5},{5,9},{9,... | collective-permute-start | bytes 393224 | tf_op jit(solution)/shard_map/ppermute | solution.py:34
  36.3 5.6 %collective-permute-start.9 = (f32[8,4,1,512]{3,2,1,0:T(1,128)S(1)}, f32[8,4,1,512]{3,2,1,0:T(1,128)S(1)}, u32[]{:S(2)}, u32[]{:S(2)}) collective-permute-start(f32[8,4,1,512]{3,2,1,0:T(1,128)S(1)} %get-tuple-element.285), channel_id=1, source_target_pairs={{0,1},{1,2},{2,3},{4,5},{5,6},{6,7},{8,9},{9,10},{10,11},{12,13},{... | collective-permute-start | bytes 196616 | tf_op jit(solution)/shard_map/ppermute | solution.py:34
  42.2 8.1 %collective-permute-start.10 = (f32[8,1,8,512]{3,2,1,0:T(8,128)S(1)}, f32[8,1,8,512]{3,2,1,0:T(8,128)S(1)}, u32[]{:S(2)}, u32[]{:S(2)}) collective-permute-start(f32[8,1,8,512]{3,2,1,0:T(8,128)S(1)} %get-tuple-element.314), channel_id=1, source_target_pairs={{4,0},{8,4},{12,8},{16,12},{20,16},{24,20},{28,24},{5,1},{9,5},{13... | collective-permute-start | bytes 393224 | tf_op jit(solution)/shard_map/ppermute | solution.py:36
  44.1 7.3 %collective-permute-start.11 = (f32[8,1,8,512]{3,2,1,0:T(8,128)S(1)}, f32[8,1,8,512]{3,2,1,0:T(8,128)S(1)}, u32[]{:S(2)}, u32[]{:S(2)}) collective-permute-start(f32[8,1,8,512]{3,2,1,0:T(8,128)S(1)} %get-tuple-element.313), channel_id=1, source_target_pairs={{0,4},{4,8},{8,12},{12,16},{16,20},{20,24},{24,28},{1,5},{5,9},{9,... | collective-permute-start | bytes 393224 | tf_op jit(solution)/shard_map/ppermute | solution.py:34
  53.5 5.6 %collective-permute-start.13 = (f32[8,4,1,512]{3,2,1,0:T(1,128)S(1)}, f32[8,4,1,512]{3,2,1,0:T(1,128)S(1)}, u32[]{:S(2)}, u32[]{:S(2)}) collective-permute-start(f32[8,4,1,512]{3,2,1,0:T(1,128)S(1)} %get-tuple-element.283), channel_id=1, source_target_pairs={{0,1},{1,2},{2,3},{4,5},{5,6},{6,7},{8,9},{9,10},{10,11},{12,13},{... | collective-permute-start | bytes 196616 | tf_op jit(solution)/shard_map/ppermute | solution.py:34
  62.0 4.7 %collective-permute-start.14 = (f32[8,128]{1,0:T(8,128)S(1)}, f32[8,128]{1,0:T(8,128)S(1)}, u32[]{:S(2)}, u32[]{:S(2)}) collective-permute-start(f32[8,128]{1,0:T(8,128)S(1)} %multiply_divide_fusion.1), channel_id=1, source_target_pairs={{0,4},{4,8},{8,12},{12,16},{16,20},{20,24},{24,28},{28,0},{1,5},{5... | collective-permute-start | bytes 12296 | tf_op jit(solution)/shard_map/ppermute | solution.py:155
  71.3 6.3 %collective-permute-start.16 = (f32[8,128]{1,0:T(8,128)S(1)}, f32[8,128]{1,0:T(8,128)S(1)}, u32[]{:S(2)}, u32[]{:S(2)}) collective-permute-start(f32[8,128]{1,0:T(8,128)S(1)} %collective-permute-done.15), channel_id=1, source_target_pairs={{0,4},{4,8},{8,12},{12,16},{16,20},{20,24},{24,28},{28,0},{1,5},{5... | collective-permute-start | bytes 12296 | tf_op jit(solution)/shard_map/ppermute | solution.py:155
  77.6 6.3 %collective-permute-start.17 = (f32[8,128]{1,0:T(8,128)S(1)}, f32[8,128]{1,0:T(8,128)S(1)}, u32[]{:S(2)}, u32[]{:S(2)}) collective-permute-start(f32[8,128]{1,0:T(8,128)S(1)} %collective-permute-done.16), channel_id=1, source_target_pairs={{0,4},{4,8},{8,12},{12,16},{16,20},{20,24},{24,28},{28,0},{1,5},{5... | collective-permute-start | bytes 12296 | tf_op jit(solution)/shard_map/ppermute | solution.py:155
  79.0 4.9 %collective-permute-start.20 = (f32[8,128]{1,0:T(8,128)S(1)}, f32[8,128]{1,0:T(8,128)S(1)}, u32[]{:S(2)}, u32[]{:S(2)}) collective-permute-start(f32[8,128]{1,0:T(8,128)S(1)} %collective-permute-done.19), channel_id=1, source_target_pairs={{4,0},{8,4},{12,8},{16,12},{20,16},{24,20},{28,24},{0,28},{5,1},{9... | collective-permute-start | bytes 12296 | tf_op jit(solution)/shard_map/ppermute | solution.py:157
  123.3 9.1 %collective-permute-start.21 = (f32[8,1,8,512]{3,2,1,0:T(8,128)S(1)}, f32[8,1,8,512]{3,2,1,0:T(8,128)S(1)}, u32[]{:S(2)}, u32[]{:S(2)}) collective-permute-start(f32[8,1,8,512]{3,2,1,0:T(8,128)S(1)} %get-tuple-element.310), channel_id=1, source_target_pairs={{4,0},{8,4},{12,8},{16,12},{20,16},{24,20},{28,24},{5,1},{9,5},{13... | collective-permute-start | bytes 393224 | tf_op jit(solution)/shard_map/ppermute | solution.py:36
  129.9 6.9 %collective-permute-start.22 = (f32[8,1,8,512]{3,2,1,0:T(8,128)S(1)}, f32[8,1,8,512]{3,2,1,0:T(8,128)S(1)}, u32[]{:S(2)}, u32[]{:S(2)}) collective-permute-start(f32[8,1,8,512]{3,2,1,0:T(8,128)S(1)} %get-tuple-element.309), channel_id=1, source_target_pairs={{0,4},{4,8},{8,12},{12,16},{16,20},{20,24},{24,28},{1,5},{5,9},{9,... | collective-permute-start | bytes 393224 | tf_op jit(solution)/shard_map/ppermute | solution.py:34
  138.8 5.6 %collective-permute-start.24 = (f32[8,4,1,512]{3,2,1,0:T(1,128)S(1)}, f32[8,4,1,512]{3,2,1,0:T(1,128)S(1)}, u32[]{:S(2)}, u32[]{:S(2)}) collective-permute-start(f32[8,4,1,512]{3,2,1,0:T(1,128)S(1)} %get-tuple-element.281), channel_id=1, source_target_pairs={{0,1},{1,2},{2,3},{4,5},{5,6},{6,7},{8,9},{9,10},{10,11},{12,13},{... | collective-permute-start | bytes 196616 | tf_op jit(solution)/shard_map/ppermute | solution.py:34
  144.7 7.8 %collective-permute-start.25 = (f32[8,1,8,512]{3,2,1,0:T(8,128)S(1)}, f32[8,1,8,512]{3,2,1,0:T(8,128)S(1)}, u32[]{:S(2)}, u32[]{:S(2)}) collective-permute-start(f32[8,1,8,512]{3,2,1,0:T(8,128)S(1)} %get-tuple-element.306), channel_id=1, source_target_pairs={{4,0},{8,4},{12,8},{16,12},{20,16},{24,20},{28,24},{5,1},{9,5},{13... | collective-permute-start | bytes 393224 | tf_op jit(solution)/shard_map/ppermute | solution.py:36
  146.6 7.3 %collective-permute-start.26 = (f32[8,1,8,512]{3,2,1,0:T(8,128)S(1)}, f32[8,1,8,512]{3,2,1,0:T(8,128)S(1)}, u32[]{:S(2)}, u32[]{:S(2)}) collective-permute-start(f32[8,1,8,512]{3,2,1,0:T(8,128)S(1)} %get-tuple-element.305), channel_id=1, source_target_pairs={{0,4},{4,8},{8,12},{12,16},{16,20},{20,24},{24,28},{1,5},{5,9},{9,... | collective-permute-start | bytes 393224 | tf_op jit(solution)/shard_map/ppermute | solution.py:34
  155.9 5.6 %collective-permute-start.28 = (f32[8,4,1,512]{3,2,1,0:T(1,128)S(1)}, f32[8,4,1,512]{3,2,1,0:T(1,128)S(1)}, u32[]{:S(2)}, u32[]{:S(2)}) collective-permute-start(f32[8,4,1,512]{3,2,1,0:T(1,128)S(1)} %get-tuple-element.279), channel_id=1, source_target_pairs={{0,1},{1,2},{2,3},{4,5},{5,6},{6,7},{8,9},{9,10},{10,11},{12,13},{... | collective-permute-start | bytes 196616 | tf_op jit(solution)/shard_map/ppermute | solution.py:34
  161.8 8.3 %collective-permute-start.29 = (f32[8,1,8,512]{3,2,1,0:T(8,128)S(1)}, f32[8,1,8,512]{3,2,1,0:T(8,128)S(1)}, u32[]{:S(2)}, u32[]{:S(2)}) collective-permute-start(f32[8,1,8,512]{3,2,1,0:T(8,128)S(1)} %get-tuple-element.302), channel_id=1, source_target_pairs={{4,0},{8,4},{12,8},{16,12},{20,16},{24,20},{28,24},{5,1},{9,5},{13... | collective-permute-start | bytes 393224 | tf_op jit(solution)/shard_map/ppermute | solution.py:36
  163.8 7.8 %collective-permute-start.30 = (f32[8,1,8,512]{3,2,1,0:T(8,128)S(1)}, f32[8,1,8,512]{3,2,1,0:T(8,128)S(1)}, u32[]{:S(2)}, u32[]{:S(2)}) collective-permute-start(f32[8,1,8,512]{3,2,1,0:T(8,128)S(1)} %get-tuple-element.301), channel_id=1, source_target_pairs={{0,4},{4,8},{8,12},{12,16},{16,20},{20,24},{24,28},{1,5},{5,9},{9,... | collective-permute-start | bytes 393224 | tf_op jit(solution)/shard_map/ppermute | solution.py:34
  173.6 5.6 %collective-permute-start.32 = (f32[8,4,1,512]{3,2,1,0:T(1,128)S(1)}, f32[8,4,1,512]{3,2,1,0:T(1,128)S(1)}, u32[]{:S(2)}, u32[]{:S(2)}) collective-permute-start(f32[8,4,1,512]{3,2,1,0:T(1,128)S(1)} %get-tuple-element.277), channel_id=1, source_target_pairs={{0,1},{1,2},{2,3},{4,5},{5,6},{6,7},{8,9},{9,10},{10,11},{12,13},{... | collective-permute-start | bytes 196616 | tf_op jit(solution)/shard_map/ppermute | solution.py:34
  179.5 8.2 %collective-permute-start.33 = (f32[8,1,8,512]{3,2,1,0:T(8,128)S(1)}, f32[8,1,8,512]{3,2,1,0:T(8,128)S(1)}, u32[]{:S(2)}, u32[]{:S(2)}) collective-permute-start(f32[8,1,8,512]{3,2,1,0:T(8,128)S(1)} %get-tuple-element.298), channel_id=1, source_target_pairs={{4,0},{8,4},{12,8},{16,12},{20,16},{24,20},{28,24},{5,1},{9,5},{13... | collective-permute-start | bytes 393224 | tf_op jit(solution)/shard_map/ppermute | solution.py:36
  181.5 7.8 %collective-permute-start.34 = (f32[8,1,8,512]{3,2,1,0:T(8,128)S(1)}, f32[8,1,8,512]{3,2,1,0:T(8,128)S(1)}, u32[]{:S(2)}, u32[]{:S(2)}) collective-permute-start(f32[8,1,8,512]{3,2,1,0:T(8,128)S(1)} %get-tuple-element.297), channel_id=1, source_target_pairs={{0,4},{4,8},{8,12},{12,16},{16,20},{20,24},{24,28},{1,5},{5,9},{9,... | collective-permute-start | bytes 393224 | tf_op jit(solution)/shard_map/ppermute | solution.py:34
  191.2 5.6 %collective-permute-start.36 = (f32[8,4,1,512]{3,2,1,0:T(1,128)S(1)}, f32[8,4,1,512]{3,2,1,0:T(1,128)S(1)}, u32[]{:S(2)}, u32[]{:S(2)}) collective-permute-start(f32[8,4,1,512]{3,2,1,0:T(1,128)S(1)} %get-tuple-element.275), channel_id=1, source_target_pairs={{0,1},{1,2},{2,3},{4,5},{5,6},{6,7},{8,9},{9,10},{10,11},{12,13},{... | collective-permute-start | bytes 196616 | tf_op jit(solution)/shard_map/ppermute | solution.py:34
  208.9 4.6 %collective-permute-start.39 = (f32[8,128]{1,0:T(8,128)S(1)}, f32[8,128]{1,0:T(8,128)S(1)}, u32[]{:S(2)}, u32[]{:S(2)}) collective-permute-start(f32[8,128]{1,0:T(8,128)S(1)} %collective-permute-done.38), channel_id=1, source_target_pairs={{0,4},{4,8},{8,12},{12,16},{16,20},{20,24},{24,28},{28,0},{1,5},{5... | collective-permute-start | bytes 12296 | tf_op jit(solution)/shard_map/ppermute | solution.py:155
  213.5 6.3 %collective-permute-start.40 = (f32[8,128]{1,0:T(8,128)S(1)}, f32[8,128]{1,0:T(8,128)S(1)}, u32[]{:S(2)}, u32[]{:S(2)}) collective-permute-start(f32[8,128]{1,0:T(8,128)S(1)} %collective-permute-done.39), channel_id=1, source_target_pairs={{0,4},{4,8},{8,12},{12,16},{16,20},{20,24},{24,28},{28,0},{1,5},{5... | collective-permute-start | bytes 12296 | tf_op jit(solution)/shard_map/ppermute | solution.py:155
  260.4 8.0 %collective-permute-start.44 = (f32[8,1,8,512]{3,2,1,0:T(8,128)S(1)}, f32[8,1,8,512]{3,2,1,0:T(8,128)S(1)}, u32[]{:S(2)}, u32[]{:S(2)}) collective-permute-start(f32[8,1,8,512]{3,2,1,0:T(8,128)S(1)} %get-tuple-element.294), channel_id=1, source_target_pairs={{4,0},{8,4},{12,8},{16,12},{20,16},{24,20},{28,24},{5,1},{9,5},{13... | collective-permute-start | bytes 393224 | tf_op jit(solution)/shard_map/ppermute | solution.py:36
  265.9 6.9 %collective-permute-start.45 = (f32[8,1,8,512]{3,2,1,0:T(8,128)S(1)}, f32[8,1,8,512]{3,2,1,0:T(8,128)S(1)}, u32[]{:S(2)}, u32[]{:S(2)}) collective-permute-start(f32[8,1,8,512]{3,2,1,0:T(8,128)S(1)} %get-tuple-element.293), channel_id=1, source_target_pairs={{0,4},{4,8},{8,12},{12,16},{16,20},{20,24},{24,28},{1,5},{5,9},{9,... | collective-permute-start | bytes 393224 | tf_op jit(solution)/shard_map/ppermute | solution.py:34
  274.7 5.6 %collective-permute-start.47 = (f32[8,4,1,512]{3,2,1,0:T(1,128)S(1)}, f32[8,4,1,512]{3,2,1,0:T(1,128)S(1)}, u32[]{:S(2)}, u32[]{:S(2)}) collective-permute-start(f32[8,4,1,512]{3,2,1,0:T(1,128)S(1)} %get-tuple-element.273), channel_id=1, source_target_pairs={{0,1},{1,2},{2,3},{4,5},{5,6},{6,7},{8,9},{9,10},{10,11},{12,13},{... | collective-permute-start | bytes 196616 | tf_op jit(solution)/shard_map/ppermute | solution.py:34
  (18 other events, 154.1 us)
